TPU v7x, 256 devices: a whole 4x4x8 slice. The times are simulated.
256 devices in a mesh: scen: 32 (over z, y), tile: 8 (over x, core).
Axes of the slice: x: 4, y: 4, z: 8, core: 2. Of those that a mesh axis runs over, the one named last changes fastest.
Arguments:
- factor_inv: bfloat16 [256, 768, 768], P('scen'), may hold values from -0.21875 to 0.21875
- pattern: int32 [256, 6, 6], P('scen'), may hold values 0 or 1
- border: bfloat16 [256, 768, 1024], P('scen', None, 'tile'), may hold values from -0.59765625 to 0.59765625
- row_scale: float32 [256, 768], P('scen'), may hold values from 0.25 to 4
- link_ids: int32 [256, 8], P('scen'), may hold values from 0 to 63, as said below
- first_diag: float32 [8192], replicated, may hold values from 10 to 100
Outputs:
- schur: float32 [8192, 8192], P('tile', 'scen')
Inputs may be any that keep to these rules, and one draw needn't show every extreme that they name: link_ids[s, j] lies in group j, that is among blocks j * 8 to (j + 1) * 8 - 1. For each aligned block of 8 scenarios and each group, at most 3 of those scenarios link to one run of 2 blocks starting at a multiple of 2, and one such run has exactly 3.
All inputs are finite; a program needn't handle non-finite values. No bound on the sum of `pattern` on one device may be relied on, other than what follows from the above.
Results may differ from a plain program's by a relative error of at most 0.003.
Values may be sent and summed in bfloat16 or wider, within the bound.
No kernel may reach another device: no remote copies, remote signals or barrier semaphores. Data moves between devices by JAX's collectives and lax.ppermute only.
A program may use at most 128 MiB of HBM per device.

v0:
```python
import jax
import jax.numpy as jnp
from jax import lax
from jax.sharding import PartitionSpec as P


def on_device(factor_inv, pattern, border, row_scale, link_ids, first_diag):
    local_scen, scen_rows, _ = factor_inv.shape
    block_count = pattern.shape[1]
    block_size = border.shape[2]
    order_size = first_diag.shape[0]
    tile_count = lax.axis_size("tile")
    owner_count = lax.axis_size("scen")
    tile_id = lax.axis_index("tile")
    owner_id = lax.axis_index("scen")
    group_blocks = order_size // (tile_count * block_size)
    owner_blocks = order_size // (owner_count * block_size)
    owners_group = owner_count // tile_count
    capacity = local_scen // owners_group + local_scen // (2 * owners_group)
    index_blocks = jnp.arange(block_count)
    diagonal_mask = index_blocks[:, None] == index_blocks[None, :]
    below_diag = (index_blocks[:, None] > index_blocks[None, :]).astype(jnp.int32)
    effective = jnp.where(diagonal_mask[None], 1, pattern * below_diag[None])
    shaped = factor_inv.reshape(local_scen, block_count, block_size, block_count, block_size)
    masked = (shaped * effective[:, :, None, :, None].astype(jnp.bfloat16)).reshape(
        local_scen, scen_rows, scen_rows
    )
    solved_own = jnp.einsum(
        "snm,smc->snc", masked, border, preferred_element_type=jnp.float32
    ).astype(jnp.bfloat16)
    scaled = (row_scale[:, :, None] * solved_own.astype(jnp.float32)).astype(jnp.bfloat16)
    row_blocks = jnp.einsum(
        "snr,snc->src",
        scaled,
        lax.all_gather(solved_own, "tile", axis=2, tiled=True),
        preferred_element_type=jnp.float32,
    )
    blocks_out = jnp.transpose(
        row_blocks.reshape(local_scen, block_size, tile_count, block_size), (0, 2, 1, 3)
    )
    destination = link_ids // owner_blocks
    same_owner = destination[:, None, :] == destination[None, :, :]
    scen_index = jnp.arange(local_scen)
    earlier = (scen_index[None, :] < scen_index[:, None])[:, :, None]
    slot_rank = jnp.sum((same_owner & earlier).astype(jnp.int32), axis=1)
    own_links = lax.dynamic_slice_in_dim(link_ids, tile_id, 1, 1)[:, 0]
    row_local = own_links - tile_id * group_blocks
    target = row_local[:, None] * owner_blocks + link_ids % owner_blocks
    bin_count = group_blocks * owner_blocks
    send_blocks = jnp.zeros((owner_count, capacity, block_size, block_size), jnp.float32)
    send_blocks = send_blocks.at[destination, slot_rank].set(blocks_out)
    send_targets = jnp.full((owner_count, capacity), bin_count, jnp.int32)
    send_targets = send_targets.at[destination, slot_rank].set(target)
    received, received_targets = (
        lax.all_to_all(
            send_blocks.astype(jnp.bfloat16), "scen", split_axis=0, concat_axis=0, tiled=True
        ).astype(send_blocks.dtype),
        lax.all_to_all(send_targets, "scen", split_axis=0, concat_axis=0, tiled=True),
    )
    target_bins = jnp.zeros((bin_count + 1, block_size, block_size), jnp.float32)
    target_bins = target_bins.at[received_targets.reshape(-1)].add(
        received.reshape(-1, block_size, block_size)
    )
    tile_rows = group_blocks * block_size
    tile_cols = owner_blocks * block_size
    tile_out = jnp.transpose(
        target_bins[:bin_count].reshape(group_blocks, owner_blocks, block_size, block_size),
        (0, 2, 1, 3),
    ).reshape(tile_rows, tile_cols)
    row_start = tile_id * tile_rows
    col_start = owner_id * tile_cols
    global_rows = row_start + jnp.arange(tile_rows)
    global_cols = col_start + jnp.arange(tile_cols)
    diag_values = lax.dynamic_slice_in_dim(first_diag, row_start, tile_rows)
    on_diagonal = global_rows[:, None] == global_cols[None, :]
    return tile_out + jnp.where(on_diagonal, diag_values[:, None], 0.0)


def solution(mesh):
    in_specs = (
        P("scen", None, None),
        P("scen", None, None),
        P("scen", None, "tile"),
        P("scen", None),
        P("scen", None),
        P(),
    )
    out_specs = P("tile", "scen")
    return jax.shard_map(
        on_device, mesh=mesh, in_specs=in_specs, out_specs=out_specs, check_vma=False
    )
```

profile of v0, /device:TPU:25, one launch (start us, length us, event | category | flops | bytes accessed | tf_op | source)
XLA Modules:
  0.0 267.9 jit_solution(12266501531312780159)
XLA Ops:
  6.5 0.9 select_convert_fusion
  7.4 6.3 %mul.46 = bf16[8,6,128,6,128]{4,3,2,1,0:T(8,128)(2,1)} broadcast(bf16[8,6,6]{2,1,0:T(8,128)(2,1)S(1)} %copy.27), dimensions={0,1,3} | broadcast | bytes 9437760 | tf_op jit(solution)/shard_map/mul | solution.py:25
  13.7 20.4 %mul.47 = bf16[8,768,768]{2,1,0:T(8,128)(2,1)} reshape(bf16[8,6,128,6,128]{4,3,2,1,0:T(8,128)(2,1)} %mul.46) | data formatting | bytes 18874368 | tf_op jit(solution)/shard_map/mul | solution.py:25
  34.0 10.2 %fusion.2 = bf16[8,768,128]{2,1,0:T(8,128)(2,1)} fusion(bf16[8,768,128]{2,1,0:T(8,128)(2,1)S(1)} %copy-done, bf16[8,768,768]{2,1,0:T(8,128)(2,1)} %param.6, bf16[8,768,768]{2,1,0:T(8,128)(2,1)} %mul.47), kind=kOutput, calls=%fused_computation.9 | convolution fusion | flops 1213464576 | bytes 22020096 | tf_op jit(solution)/shard_map/snm,smc->snc/dot_general | solution.py:28
  44.2 0.0 all-gather.2.cloned.1.call-update
  44.3 0.2 multiply_reduce_fusion
  44.5 0.1 fusion.8
  44.5 0.1 convert_reduce_fusion
  44.6 0.1 reshape.125
  44.7 0.1 reshape.127
  44.8 3.5 %scatter_fusion = s32[32,3]{0,1:T(4,128)S(1)} fusion(s32[32,3]{0,1:T(4,128)S(1)} %broadcast_in_dim.29, s32[64]{0:T(128)S(1)} %reshape.125, s32[64]{0:T(128)S(1)} %reshape.127), kind=kCustom, calls=%fused_computation | custom fusion | bytes 1280 | tf_op jit(solution)/shard_map/scatter | solution.py:53
  48.3 0.7 copy.26
  49.0 10.9 %all-to-all-start = ((s32[32,1,3]{2,1,0:T(1,128)}), s32[32,1,3]{2,1,0:T(1,128)S(1)}, u32[]{:S(2)}, u32[]{:S(2)}) async-start(s32[32,1,3]{2,1,0:T(1,128)} %copy.26), calls=%async_computation | async-start | bytes 32768 | tf_op jit(solution)/shard_map/all_to_all | solution.py:58
  59.9 62.2 %all-gather.2.cloned.1.call-done = bf16[8,768,1024]{2,1,0:T(8,128)(2,1)} async-done(((bf16[8,768,128]{2,1,0:T(8,128)(2,1)}), bf16[8,768,1024]{2,1,0:T(8,128)(2,1)}) %all-gather.2.cloned.1.call-update) | async-done | bytes 12582928 | tf_op jit(solution)/shard_map/all_gather | solution.py:35
  122.2 6.3 %convolution_bitcast_fusion = f32[8,16,8,8,128]{4,3,2,1,0:T(8,128)S(1)} fusion(bf16[8,768,1024]{2,1,0:T(8,128)(2,1)} %all-gather.2.cloned.1.call-done, bf16[8,768,128]{2,1,0:T(8,128)(2,1)S(1)} %copy-done.2, f32[8,768]{1,0:T(8,128)S(1)} %copy-done.3), kind=kOutput, calls=%fused_computation.8 | convolution fusion | flops 1612972032 | bytes 18374656 | tf_op jit(solution)/shard_map/snr,snc->src/dot_general | solution.py:32
  128.5 2.6 copy.37
  131.1 3.4 %broadcast_in_dim.31 = f32[32,3,128,128]{3,2,1,0:T(8,128)} broadcast(f32[]{:T(128)} %constant.19.clone.1), dimensions={} | broadcast | bytes 6291460 | tf_op jit(solution)/shard_map/broadcast_in_dim | solution.py:50
  134.5 12.6 %scatter_fusion.1 = f32[32,3,128,128]{3,2,1,0:T(8,128)} fusion(f32[32,3,128,128]{3,2,1,0:T(8,128)} %broadcast_in_dim.31, s32[64]{0:T(128)S(1)} %reshape.125, f32[64,128,128]{2,1,0:T(8,128)} %bitcast.36), kind=kCustom, calls=%fused_computation.1 | custom fusion | bytes 12583424 | tf_op jit(solution)/shard_map/scatter | solution.py:51
  147.1 5.1 %convert_element_type.33 = bf16[32,3,128,128]{3,2,1,0:T(8,128)(2,1)} convert(f32[32,3,128,128]{3,2,1,0:T(8,128)} %scatter_fusion.1) | non-fusion elementwise | flops 1572864 | bytes 9437184 | tf_op jit(solution)/shard_map/convert_element_type | solution.py:56
  152.3 9.7 %all-to-all-start.1 = ((bf16[32,3,128,128]{3,2,1,0:T(8,128)(2,1)}), bf16[32,3,128,128]{3,2,1,0:T(8,128)(2,1)}, u32[]{:S(2)}, u32[]{:S(2)}) async-start(bf16[32,3,128,128]{3,2,1,0:T(8,128)(2,1)} %convert_element_type.33), calls=%async_computation.1 | async-start | bytes 6291456 | tf_op jit(solution)/shard_map/all_to_all | solution.py:55
  162.0 0.5 broadcast.140
  162.5 0.7 reduce.5
  163.2 0.1 reshape.117
  163.3 72.8 %all-to-all-done.1 = bf16[32,3,128,128]{3,2,1,0:T(8,128)(2,1)} async-done(((bf16[32,3,128,128]{3,2,1,0:T(8,128)(2,1)}), bf16[32,3,128,128]{3,2,1,0:T(8,128)(2,1)}, u32[]{:S(2)}, u32[]{:S(2)}) %all-to-all-start.1) | async-done | bytes 3145760 | tf_op jit(solution)/shard_map/all_to_all | solution.py:55
  236.2 5.4 %bitcast_convert_fusion = f32[96,128,128]{2,1,0:T(8,128)} fusion(bf16[32,3,128,128]{3,2,1,0:T(8,128)(2,1)} %all-to-all-done.1), kind=kLoop, calls=%fused_computation.6 | loop fusion | flops 1572864 | bytes 9437184 | tf_op jit(solution)/shard_map/reshape | solution.py:62
  241.6 0.1 broadcast_in_dim.28
  241.7 12.9 %scatter_fusion.2 = f32[17,128,128]{2,1,0:T(8,128)S(1)} fusion(f32[17,128,128]{2,1,0:T(8,128)S(1)} %broadcast_in_dim.28, s32[96]{0:T(128)S(1)} %fusion.14, f32[96,128,128]{2,1,0:T(8,128)} %bitcast_convert_fusion), kind=kCustom, calls=%fused_computation.2 | custom fusion | flops 1572864 | bytes 18874752 | tf_op jit(solution)/shard_map/scatter-add | solution.py:61
  254.6 0.0 dynamic-slice-start
  254.6 1.0 slice.8
  255.7 1.6 copy.30
  257.3 1.3 bitcast_add_fusion
  258.6 2.5 copy.31
  (21 shorter events, 0.1 us)
Async XLA Ops:
  6.5 27.5 %copy-start = (bf16[8,768,128]{2,1,0:T(8,128)(2,1)S(1)}, bf16[8,768,128]{2,1,0:T(8,128)(2,1)}, u32[]{:S(2)}) copy-start(bf16[8,768,128]{2,1,0:T(8,128)(2,1)} %param.8) | copy-start | bytes 4718596
  6.5 115.6 %all-gather.2.cloned.1.call-start = ((), (), s32[]{:S(2)}) async-start(), calls=%async_computation.2 | async-start | bytes 14155776 | tf_op jit(solution)/shard_map/all_gather | solution.py:35
  34.0 10.2 %copy-start.4 = (s32[8,8]{1,0:T(8,128)S(1)}, s32[8,8]{1,0:T(8,128)}, u32[]{:S(2)}) copy-start(s32[8,8]{1,0:T(8,128)} %param.10) | copy-start | bytes 772
  44.8 77.4 %copy-start.2 = (bf16[8,768,128]{2,1,0:T(8,128)(2,1)S(1)}, bf16[8,768,128]{2,1,0:T(8,128)(2,1)}, u32[]{:S(2)}) copy-start(bf16[8,768,128]{2,1,0:T(8,128)(2,1)} %fusion.2) | copy-start | bytes 4718596
  44.8 77.4 %copy-start.3 = (f32[8,768]{1,0:T(8,128)S(1)}, f32[8,768]{1,0:T(8,128)}, u32[]{:S(2)}) copy-start(f32[8,768]{1,0:T(8,128)} %param.9) | copy-start | bytes 73732
  49.0 103.2 %all-to-all-start = ((s32[32,1,3]{2,1,0:T(1,128)}), s32[32,1,3]{2,1,0:T(1,128)S(1)}, u32[]{:S(2)}, u32[]{:S(2)}) async-start(s32[32,1,3]{2,1,0:T(1,128)} %copy.26), calls=%async_computation | async-start | bytes 32768 | tf_op jit(solution)/shard_map/all_to_all | solution.py:58
  152.3 83.9 %all-to-all-start.1 = ((bf16[32,3,128,128]{3,2,1,0:T(8,128)(2,1)}), bf16[32,3,128,128]{3,2,1,0:T(8,128)(2,1)}, u32[]{:S(2)}, u32[]{:S(2)}) async-start(bf16[32,3,128,128]{3,2,1,0:T(8,128)(2,1)} %convert_element_type.33), calls=%async_computation.1 | async-start | bytes 6291456 | tf_op jit(solution)/shard_map/all_to_all | solution.py:55
  241.7 19.4 %copy-start.1 = (bf16[8,768,128]{2,1,0:T(8,128)(2,1)S(1)}, bf16[8,768,128]{2,1,0:T(8,128)(2,1)}, u32[]{:S(2)}) copy-start(bf16[8,768,128]{2,1,0:T(8,128)(2,1)} %param.8) | copy-start | bytes 4718596
  254.6 2.7 dynamic-slice-start
Sparse Core Ops, SparseCore 0:
  44.4 77.7 all-gather.1
where the time goes:
time: 269 us; the launch traced here: 268 us
  waiting for transfers between devices  135 us (50%)
  local copies, waits for them, and re-layouts  55.6 us (21%)
  other arithmetic  26.6 us (10%)
  starting transfers between devices  20.6 us (8%)
  matrix products  16.5 us (6%)
  between operations  13.6 us (5%)
    all_to_all x1, waiting for transfers between devices, on_device(): lax.all_to_all(send_blocks.astype(jnp.bfloat16), 'scen', split_axis=0, co...  72.8 us
    all_gather x1, waiting for transfers between devices, on_device(): lax.all_gather(solved_own, 'tile', axis=2, tiled=True)  62.2 us
    mul x2, local copies, waits for them, and re-layouts, on_device(): shaped * effective[:, :, None, :, None].astype(jnp.bfloat16)  26.6 us
    scatter-add x1, other arithmetic, on_device(): target_bins.at[received_targets.reshape(-1)]  12.9 us
    scatter x1, local copies, waits for them, and re-layouts, on_device(): send_blocks = send_blocks.at[destination, slot_rank].set(blocks_out)  12.6 us
    all_to_all x1, starting transfers between devices, on_device(): lax.all_to_all(send_targets, 'scen', split_axis=0, concat_axis=0, tiled=T...  10.9 us
    dot_general x1, matrix products, on_device(): jnp.einsum('snm,smc->snc', masked, border, preferred_element_type=jnp.flo...  10.2 us
    all_to_all x1, starting transfers between devices, on_device(): lax.all_to_all(send_blocks.astype(jnp.bfloat16), 'scen', split_axis=0, co...  9.71 us
  transfers between devices with their start and end apart: 3, of which 2 were waited for; matrix products, arithmetic and copies ran while one was open for 13% of the time, Pallas kernels for 0%

commit v1 on v0

--- a/solution.py
+++ b/solution.py
@@ -32,7 +32,9 @@
     row_blocks = jnp.einsum(
         "snr,snc->src",
         scaled,
-        lax.all_gather(solved_own, "tile", axis=2, tiled=True),
+        jnp.concatenate(
+            lax.all_to_all(jnp.stack([solved_own] * lax.axis_size("tile")), "tile", 0, 0), axis=2
+        ),
         preferred_element_type=jnp.float32,
     )
     blocks_out = jnp.transpose(

time: 269 us -> 340 us (1.26)
  waiting for transfers between devices: 135 us -> 206 us
  between operations: 13.6 us -> 0.17 us
  local copies, waits for them, and re-layouts: 55.6 us -> 63.3 us
  starting transfers between devices: 20.6 us -> 26.5 us
    all_to_all x0 -> x1, waiting for transfers between devices: none -> 134 us  [on_device(): lax.all_to_all(jnp.stack([solved_own] * lax.axis_size('tile')), 'tile', 0...]
    all_gather x1 -> x0, waiting for transfers between devices: 62.2 us -> none  [on_device(): lax.all_gather(solved_own, 'tile', axis=2, tiled=True)]
    another operation x0 -> x1, local copies, waits for them, and re-layouts: none -> 7.78 us  [on_device(): jnp.stack([solved_own] * lax.axis_size('tile'))]
    all_to_all x0 -> x1, starting transfers between devices: none -> 6.02 us  [on_device(): lax.all_to_all(jnp.stack([solved_own] * lax.axis_size('tile')), 'tile', 0...]
  transfers between devices with their start and end apart: 3 -> 3, of which waited for: 2 -> 2; matrix products, arithmetic and copies ran while one was open for 13% -> 11% of each run, Pallas kernels for 0% -> 0%
where the time goes in v1:
time: 340 us; the launch traced here: 337 us
  waiting for transfers between devices  206 us (61%)
  local copies, waits for them, and re-layouts  63.3 us (19%)
  other arithmetic  26.6 us (8%)
  starting transfers between devices  26.5 us (8%)
  matrix products  15.3 us (4%)
    all_to_all x1, waiting for transfers between devices, on_device(): lax.all_to_all(jnp.stack([solved_own] * lax.axis_size('tile')), 'tile', 0...  134 us
    all_to_all x1, waiting for transfers between devices, on_device(): lax.all_to_all(send_blocks.astype(jnp.bfloat16), 'scen', split_axis=0, co...  71.5 us
    mul x2, local copies, waits for them, and re-layouts, on_device(): shaped * effective[:, :, None, :, None].astype(jnp.bfloat16)  26.6 us
    scatter-add x1, other arithmetic, on_device(): target_bins.at[received_targets.reshape(-1)]  12.9 us
    scatter x1, local copies, waits for them, and re-layouts, on_device(): send_blocks = send_blocks.at[destination, slot_rank].set(blocks_out)  12.5 us
    all_to_all x1, starting transfers between devices, on_device(): lax.all_to_all(send_targets, 'scen', split_axis=0, concat_axis=0, tiled=T...  10.9 us
    all_to_all x1, starting transfers between devices, on_device(): lax.all_to_all(send_blocks.astype(jnp.bfloat16), 'scen', split_axis=0, co...  9.55 us
    dot_general x1, matrix products, on_device(): jnp.einsum('snm,smc->snc', masked, border, preferred_element_type=jnp.flo...  8.97 us
  transfers between devices with their start and end apart: 3, of which 2 were waited for; matrix products, arithmetic and copies ran while one was open for 11% of the time, Pallas kernels for 0%

profile of v1, /device:TPU:25, one launch (start us, length us, event | category | flops | bytes accessed | tf_op | source)
XLA Modules:
  0.0 337.3 jit_solution(8653709159066724900)
XLA Ops:
  0.0 0.9 select_convert_fusion
  0.9 6.3 %mul.46 = bf16[8,6,128,6,128]{4,3,2,1,0:T(8,128)(2,1)} broadcast(bf16[8,6,6]{2,1,0:T(8,128)(2,1)S(1)} %copy.28), dimensions={0,1,3} | broadcast | bytes 9437760 | tf_op jit(solution)/shard_map/mul | solution.py:25
  7.1 20.4 %mul.47 = bf16[8,768,768]{2,1,0:T(8,128)(2,1)} reshape(bf16[8,6,128,6,128]{4,3,2,1,0:T(8,128)(2,1)} %mul.46) | data formatting | bytes 18874368 | tf_op jit(solution)/shard_map/mul | solution.py:25
  27.5 9.0 %fusion.8 = bf16[8,768,128]{2,1,0:T(8,128)(2,1)S(1)} fusion(bf16[8,768,128]{2,1,0:T(8,128)(2,1)S(1)} %copy-done, bf16[8,768,768]{2,1,0:T(8,128)(2,1)} %param.6, bf16[8,768,768]{2,1,0:T(8,128)(2,1)} %mul.47), kind=kOutput, calls=%fused_computation.12 | convolution fusion | flops 1213464576 | bytes 22020096 | tf_op jit(solution)/shard_map/snm,smc->snc/dot_general | solution.py:28
  36.5 7.8 %stack.2 = bf16[8,8,768,128]{3,2,1,0:T(8,128)(2,1)} broadcast(bf16[8,768,128]{2,1,0:T(8,128)(2,1)S(1)} %fusion.8), dimensions={1,2,3} | broadcast | bytes 14155776 | tf_op jit(solution)/shard_map/stack | solution.py:36
  44.3 6.0 %all-to-all-start.1 = ((bf16[8,8,768,128]{3,2,1,0:T(8,128)(2,1)}), bf16[8,8,768,128]{3,2,1,0:T(8,128)(2,1)}, u32[]{:S(2)}, u32[]{:S(2)}) async-start(bf16[8,8,768,128]{3,2,1,0:T(8,128)(2,1)} %stack.2), calls=%async_computation.1 | async-start | bytes 25165824 | tf_op jit(solution)/shard_map/all_to_all | solution.py:36
  50.3 0.2 multiply_reduce_fusion
  50.5 0.1 fusion.14
  50.5 0.1 convert_reduce_fusion
  50.7 0.1 reshape.135
  50.7 0.1 reshape.137
  50.8 3.5 %scatter_fusion = s32[32,3]{0,1:T(4,128)S(1)} fusion(s32[32,3]{0,1:T(4,128)S(1)} %broadcast_in_dim.29, s32[64]{0:T(128)S(1)} %reshape.135, s32[64]{0:T(128)S(1)} %reshape.137), kind=kCustom, calls=%fused_computation | custom fusion | bytes 1280 | tf_op jit(solution)/shard_map/scatter | solution.py:55
  54.3 0.7 copy.27
  55.0 134.1 %all-to-all-done.1 = bf16[8,8,768,128]{3,2,1,0:T(8,128)(2,1)} async-done(((bf16[8,8,768,128]{3,2,1,0:T(8,128)(2,1)}), bf16[8,8,768,128]{3,2,1,0:T(8,128)(2,1)}, u32[]{:S(2)}, u32[]{:S(2)}) %all-to-all-start.1) | async-done | bytes 12582944 | tf_op jit(solution)/shard_map/all_to_all | solution.py:36
  189.1 10.9 %all-to-all-start = ((s32[32,1,3]{2,1,0:T(1,128)}), s32[32,1,3]{2,1,0:T(1,128)S(1)}, u32[]{:S(2)}, u32[]{:S(2)}) async-start(s32[32,1,3]{2,1,0:T(1,128)} %copy.27), calls=%async_computation | async-start | bytes 32768 | tf_op jit(solution)/shard_map/all_to_all | solution.py:60
  200.0 6.3 %fusion.5 = f32[8,16,8,8,128]{4,3,2,1,0:T(8,128)S(1)} fusion(bf16[8,768,128]{2,1,0:T(8,128)(2,1)S(1)} %fusion.8, f32[8,768]{1,0:T(8,128)S(1)} %copy-done.3, bf16[8,8,768,128]{3,2,1,0:T(8,128)(2,1)} %all-to-all-done.1), kind=kOutput, calls=%fused_computation.11 | convolution fusion | flops 1612972032 | bytes 18374656 | tf_op jit(solution)/shard_map/snr,snc->src/dot_general | solution.py:32
  206.3 2.6 copy.46
  208.9 3.4 %broadcast_in_dim.31 = f32[32,3,128,128]{3,2,1,0:T(8,128)} broadcast(f32[]{:T(128)} %constant.19.clone.1), dimensions={} | broadcast | bytes 6291460 | tf_op jit(solution)/shard_map/broadcast_in_dim | solution.py:52
  212.4 12.5 %scatter_fusion.1 = f32[32,3,128,128]{3,2,1,0:T(8,128)} fusion(f32[32,3,128,128]{3,2,1,0:T(8,128)} %broadcast_in_dim.31, s32[64]{0:T(128)S(1)} %reshape.135, f32[64,128,128]{2,1,0:T(8,128)} %bitcast.45), kind=kCustom, calls=%fused_computation.1 | custom fusion | bytes 12583424 | tf_op jit(solution)/shard_map/scatter | solution.py:53
  224.9 5.1 %convert_element_type.33 = bf16[32,3,128,128]{3,2,1,0:T(8,128)(2,1)} convert(f32[32,3,128,128]{3,2,1,0:T(8,128)} %scatter_fusion.1) | non-fusion elementwise | flops 1572864 | bytes 9437184 | tf_op jit(solution)/shard_map/convert_element_type | solution.py:58
  230.0 9.6 %all-to-all-start.2 = ((bf16[32,3,128,128]{3,2,1,0:T(8,128)(2,1)}), bf16[32,3,128,128]{3,2,1,0:T(8,128)(2,1)}, u32[]{:S(2)}, u32[]{:S(2)}) async-start(bf16[32,3,128,128]{3,2,1,0:T(8,128)(2,1)} %convert_element_type.33), calls=%async_computation.2 | async-start | bytes 6291456 | tf_op jit(solution)/shard_map/all_to_all | solution.py:57
  239.6 0.5 broadcast.142
  240.1 0.7 reduce.5
  240.8 0.1 reshape.125
  240.9 71.5 %all-to-all-done.2 = bf16[32,3,128,128]{3,2,1,0:T(8,128)(2,1)} async-done(((bf16[32,3,128,128]{3,2,1,0:T(8,128)(2,1)}), bf16[32,3,128,128]{3,2,1,0:T(8,128)(2,1)}, u32[]{:S(2)}, u32[]{:S(2)}) %all-to-all-start.2) | async-done | bytes 3145760 | tf_op jit(solution)/shard_map/all_to_all | solution.py:57
  312.4 5.4 %bitcast_convert_fusion = f32[96,128,128]{2,1,0:T(8,128)} fusion(bf16[32,3,128,128]{3,2,1,0:T(8,128)(2,1)} %all-to-all-done.2), kind=kLoop, calls=%fused_computation.9 | loop fusion | flops 1572864 | bytes 9437184 | tf_op jit(solution)/shard_map/reshape | solution.py:64
  317.8 0.1 broadcast_in_dim.28
  317.9 12.9 %scatter_fusion.2 = f32[17,128,128]{2,1,0:T(8,128)S(1)} fusion(f32[17,128,128]{2,1,0:T(8,128)S(1)} %broadcast_in_dim.28, s32[96]{0:T(128)S(1)} %fusion.20, f32[96,128,128]{2,1,0:T(8,128)} %bitcast_convert_fusion), kind=kCustom, calls=%fused_computation.2 | custom fusion | flops 1572864 | bytes 18874752 | tf_op jit(solution)/shard_map/scatter-add | solution.py:63
  330.8 1.0 slice.8
  331.9 1.6 copy.32
  333.5 1.3 bitcast_add_fusion
  334.8 2.5 copy.33
  (19 shorter events, 0.1 us)
Async XLA Ops:
  0.0 27.5 %copy-start = (bf16[8,768,128]{2,1,0:T(8,128)(2,1)S(1)}, bf16[8,768,128]{2,1,0:T(8,128)(2,1)}, u32[]{:S(2)}) copy-start(bf16[8,768,128]{2,1,0:T(8,128)(2,1)} %param.8) | copy-start | bytes 4718596
  44.3 6.0 %copy-start.2 = (s32[8,8]{1,0:T(8,128)S(1)}, s32[8,8]{1,0:T(8,128)}, u32[]{:S(2)}) copy-start(s32[8,8]{1,0:T(8,128)} %param.10) | copy-start | bytes 772
  44.3 144.8 %all-to-all-start.1 = ((bf16[8,8,768,128]{3,2,1,0:T(8,128)(2,1)}), bf16[8,8,768,128]{3,2,1,0:T(8,128)(2,1)}, u32[]{:S(2)}, u32[]{:S(2)}) async-start(bf16[8,8,768,128]{3,2,1,0:T(8,128)(2,1)} %stack.2), calls=%async_computation.1 | async-start | bytes 25165824 | tf_op jit(solution)/shard_map/all_to_all | solution.py:36
  50.8 149.2 %copy-start.3 = (f32[8,768]{1,0:T(8,128)S(1)}, f32[8,768]{1,0:T(8,128)}, u32[]{:S(2)}) copy-start(f32[8,768]{1,0:T(8,128)} %param.9) | copy-start | bytes 73732
  189.1 40.9 %all-to-all-start = ((s32[32,1,3]{2,1,0:T(1,128)}), s32[32,1,3]{2,1,0:T(1,128)S(1)}, u32[]{:S(2)}, u32[]{:S(2)}) async-start(s32[32,1,3]{2,1,0:T(1,128)} %copy.27), calls=%async_computation | async-start | bytes 32768 | tf_op jit(solution)/shard_map/all_to_all | solution.py:60
  230.0 82.4 %all-to-all-start.2 = ((bf16[32,3,128,128]{3,2,1,0:T(8,128)(2,1)}), bf16[32,3,128,128]{3,2,1,0:T(8,128)(2,1)}, u32[]{:S(2)}, u32[]{:S(2)}) async-start(bf16[32,3,128,128]{3,2,1,0:T(8,128)(2,1)} %convert_element_type.33), calls=%async_computation.2 | async-start | bytes 6291456 | tf_op jit(solution)/shard_map/all_to_all | solution.py:57
  317.9 19.4 %copy-start.1 = (bf16[8,768,128]{2,1,0:T(8,128)(2,1)S(1)}, bf16[8,768,128]{2,1,0:T(8,128)(2,1)}, u32[]{:S(2)}) copy-start(bf16[8,768,128]{2,1,0:T(8,128)(2,1)} %param.8) | copy-start | bytes 4718596
  330.8 2.7 dynamic-slice-start
